TPU v7x, 32 devices: a whole 2x2x4 slice. The times are simulated.
32 devices in a mesh: blk: 8 (over y, x, core), pitch: 4 (over z).
Axes of the slice: x: 2, y: 2, z: 4, core: 2. Of those that a mesh axis runs over, the one named last changes fastest.
Arguments:
- flow_state: float32 [5, 32, 128, 128], P(None, 'pitch', 'blk'), may hold values from -0.6 to 3.2, as said below
- prior_state: float32 [5, 32, 128, 128], P(None, 'pitch', 'blk'), may hold values from -0.75 to 3.35, as said below
- fourier_store: float32 [2, 49, 10, 128, 128], P(None, None, None, ('blk', 'pitch')), may hold values from -0.15 to 2.6, as said below
- sample_times: int32 [2, 128, 128], P(None, ('blk', 'pitch')), may hold values from 0 to 95
- harmonics: int32 [128, 128], P(('blk', 'pitch')), may hold values from 12 to 24
Outputs:
- new_state: float32 [5, 32, 128, 128], P(None, 'pitch', 'blk')
- new_store: float32 [2, 49, 10, 128, 128], P(None, None, None, ('blk', 'pitch'))
- new_ghosts: float32 [2, 10, 128, 128], P(None, None, ('blk', 'pitch'))
Inputs may be any that keep to these rules, and one draw needn't show every extreme that they name: `flow_state`: density between 0.7 and 1.3, momenta between -0.6 and 0.6, total energy between 2.2 and 3.2. `prior_state`: each entry within 0.15 of flow_state's. `fourier_store`: the k-th cosine and sine coefficients are at most 0.08 / k in magnitude.
All inputs are finite; a program needn't handle non-finite values.
Results may differ from a plain program's by a relative error of at most 0.000068.
Values sent between devices are 32-bit elements; how exact they have to be, the bound alone decides.
No kernel may reach another device: no remote copies, remote signals or barrier semaphores. Data moves between devices by JAX's collectives and lax.ppermute only.
A program may use at most 64 MiB of HBM per device.

v0:
```python
import math
import jax
import jax.numpy as jnp
from jax import lax
from jax.sharding import PartitionSpec as P

NT = 96
gamma_less = 0.4
diss_coeff = 0.03125
section_coefs = (1.0 / 3.0, 0.5, 1.0)
pseudo_step = 0.1
physical_step = 0.25
relax_rate = 0.125
lag_turns = 0.3


def padded_2(block, sides, width):
    for axis, dim in sides:
        count = lax.axis_size(axis)
        forward = [(i, i + 1) for i in range(count - 1)]
        backward = [(target, source) for source, target in forward]
        low = lax.ppermute(
            lax.slice_in_dim(block, block.shape[dim] - width, None, axis=dim), axis, forward
        )
        high = lax.ppermute(lax.slice_in_dim(block, 0, width, axis=dim), axis, backward)
        block = jnp.concatenate([low, block, high], axis=dim)
    return block


def fluxes(current, direction):
    density = current[0]
    velocity = current[direction] / density
    pressure = gamma_less * (
        current[4]
        - 0.5
        * (current[1] * current[1] + current[2] * current[2] + current[3] * current[3])
        / density
    )
    flux_parts = [
        current[direction],
        current[1] * velocity,
        current[2] * velocity,
        current[3] * velocity,
        (current[4] + pressure) * velocity,
    ]
    flux_parts[direction] = flux_parts[direction] + pressure
    return jnp.stack(flux_parts)


def face_sum(padded, direction):
    cells_n = padded.shape[direction] - 4
    faces_n = cells_n + 1
    cell_flux = fluxes(padded, direction)

    def window(values, offset, length):
        return lax.slice_in_dim(values, offset, offset + length, axis=direction)

    face_flux = 0.5 * (
        window(cell_flux, 1, faces_n) + window(cell_flux, 2, faces_n)
    ) - diss_coeff * (
        window(padded, 3, faces_n)
        - 3.0 * window(padded, 2, faces_n)
        + 3.0 * window(padded, 1, faces_n)
        - window(padded, 0, faces_n)
    )
    return window(face_flux, 1, cells_n) - window(face_flux, 0, cells_n)


def harmonic_tables(phases_at, harm_count):
    orders = jnp.arange(1, harm_count + 1).astype(jnp.float32).reshape((harm_count, 1, 1))
    angles = orders * phases_at[None]
    return (jnp.cos(angles), jnp.sin(angles))


def rebuild(coeffs, phases_at, active):
    harm_count = (coeffs.shape[0] - 1) // 2
    cosines, sines = harmonic_tables(phases_at, harm_count)
    orders = jnp.arange(1, harm_count + 1).reshape((harm_count, 1, 1))
    active_mask = (orders <= active[None]).astype(jnp.float32)
    harm_terms = (
        coeffs[1 : harm_count + 1] * (active_mask * cosines)[:, None]
        + coeffs[harm_count + 1 :] * (active_mask * sines)[:, None]
    )
    return coeffs[0] + jnp.sum(harm_terms, axis=0)


def refresh(coeffs, samples, phases_at):
    harm_count = (coeffs.shape[0] - 1) // 2
    cosines, sines = harmonic_tables(phases_at, harm_count)
    mean_part = (1.0 - relax_rate) * coeffs[0] + relax_rate * samples
    cos_part = (1.0 - relax_rate) * coeffs[1 : harm_count + 1] + 2.0 * relax_rate * samples[
        None
    ] * cosines[:, None]
    sin_part = (1.0 - relax_rate) * coeffs[harm_count + 1 :] + 2.0 * relax_rate * samples[
        None
    ] * sines[:, None]
    return jnp.concatenate([mean_part[None], cos_part, sin_part], axis=0)


def shards(flow_state, prior_state, fourier_store, sample_times, harmonics):
    pitch_at = lax.axis_index("pitch")
    pitch_end = lax.axis_size("pitch") - 1
    blk_at = lax.axis_index("blk")
    blk_end = lax.axis_size("blk") - 1
    block_rows = flow_state.shape[2]
    radial_cells = flow_state.shape[3]
    period = 2.0 * math.pi / NT
    phase_lag = 2.0 * math.pi * lag_turns
    phases = sample_times.astype(jnp.float32) * period
    low_share = rebuild(fourier_store[0], phases[0] - phase_lag, harmonics)
    high_share = rebuild(fourier_store[1], phases[1] + phase_lag, harmonics)
    low_whole, high_whole = (
        lax.all_gather(low_share, "pitch", axis=1, tiled=True),
        lax.all_gather(high_share, "pitch", axis=1, tiled=True),
    )
    ghost_shape = (5, 2, block_rows, radial_cells)
    low_ghost = low_whole.reshape(ghost_shape)
    high_ghost = high_whole.reshape(ghost_shape)
    current = flow_state
    for section_coef in section_coefs:
        pitch_pad = padded_2(current, (("pitch", 1),), 2)
        axial_pad = padded_2(current, (("blk", 2),), 2)
        pitch_pad = jnp.concatenate(
            [
                jnp.where(pitch_at == 0, low_ghost, pitch_pad[:, :2]),
                current,
                jnp.where(pitch_at == pitch_end, high_ghost, pitch_pad[:, -2:]),
            ],
            axis=1,
        )
        lower_edge = jnp.broadcast_to(current[:, :, :1], axial_pad[:, :, :2].shape)
        upper_edge = jnp.broadcast_to(current[:, :, -1:], axial_pad[:, :, :2].shape)
        axial_pad = jnp.concatenate(
            [
                jnp.where(blk_at == 0, lower_edge, axial_pad[:, :, :2]),
                current,
                jnp.where(blk_at == blk_end, upper_edge, axial_pad[:, :, -2:]),
            ],
            axis=2,
        )
        radial_pad = jnp.pad(current, ((0, 0), (0, 0), (0, 0), (2, 2)), mode="edge")
        summed = face_sum(pitch_pad, 1) + face_sum(axial_pad, 2) + face_sum(radial_pad, 3)
        summed = summed + (3.0 * current - 4.0 * flow_state + prior_state) * (0.5 / physical_step)
        current = flow_state - section_coef * pseudo_step * summed
    face_shape = (10, block_rows, radial_cells)
    upper_face = current[:, -2:].reshape(face_shape)
    lower_face = current[:, :2].reshape(face_shape)
    nothing = jnp.zeros_like(lower_face)
    upper_mine, lower_mine = (
        lax.psum_scatter(
            jnp.where(pitch_at == pitch_end, upper_face, nothing),
            "pitch",
            scatter_dimension=1,
            tiled=True,
        ),
        lax.psum_scatter(
            jnp.where(pitch_at == 0, lower_face, nothing), "pitch", scatter_dimension=1, tiled=True
        ),
    )
    next_phases = phases + period
    low_store = refresh(fourier_store[0], upper_mine, next_phases[0])
    high_store = refresh(fourier_store[1], lower_mine, next_phases[1])
    ghosts = jnp.stack(
        [
            rebuild(low_store, next_phases[0] - phase_lag, harmonics),
            rebuild(high_store, next_phases[1] + phase_lag, harmonics),
        ]
    )
    return (current, jnp.stack([low_store, high_store]), ghosts)


def solution(mesh):
    placed = (
        P(None, "pitch", "blk", None),
        P(None, "pitch", "blk", None),
        P(None, None, None, ("blk", "pitch"), None),
        P(None, ("blk", "pitch"), None),
        P(("blk", "pitch"), None),
    )
    return jax.shard_map(
        shards,
        mesh=mesh,
        in_specs=placed,
        out_specs=(
            P(None, "pitch", "blk", None),
            P(None, None, None, ("blk", "pitch"), None),
            P(None, None, ("blk", "pitch"), None),
        ),
        check_vma=False,
    )
```

profile of v0, /device:TPU:0, one launch (start us, length us, event | category | flops | bytes accessed | tf_op | source)
XLA Modules:
  0.0 152.5 jit_solution(4150837358878901428)
XLA Ops:
  7.2 1.7 %fusion.114 = (f32[5,8,2,128]{3,2,1,0:T(2,128)}, f32[5,8,2,128]{3,2,1,0:T(2,128)}) fusion(f32[5,8,16,128]{3,2,1,0:T(8,128)} %param.5), kind=kLoop, calls=%fused_computation.305 | loop fusion | bytes 163840 | tf_op jit(solution)/shard_map/slice | solution.py:25
  8.9 3.0 %collective-permute-start.2 = (f32[5,8,2,128]{3,2,1,0:T(2,128)}, f32[5,8,2,128]{3,2,1,0:T(2,128)}, u32[]{:S(2)}, u32[]{:S(2)}) collective-permute-start(f32[5,8,2,128]{3,2,1,0:T(2,128)} %get-tuple-element.86), channel_id=1, source_target_pairs={{0,4},{4,8},{8,12},{12,16},{16,20},{20,24},{24,28},{1,5},{5,9},{9,... | collective-permute-start | bytes 122888 | tf_op jit(solution)/shard_map/ppermute | solution.py:22
  11.9 1.3 collective-permute-start.3
  13.2 1.6 %fusion.112 = (f32[5,2,16,128]{3,2,1,0:T(8,128)}, f32[5,2,16,128]{3,2,1,0:T(8,128)}) fusion(f32[5,8,16,128]{3,2,1,0:T(8,128)} %param.5), kind=kLoop, calls=%fused_computation.303 | loop fusion | bytes 327680 | tf_op jit(solution)/shard_map/slice | solution.py:25
  14.8 4.9 %collective-permute-start = (f32[5,2,16,128]{3,2,1,0:T(8,128)}, f32[5,2,16,128]{3,2,1,0:T(8,128)}, u32[]{:S(2)}, u32[]{:S(2)}) collective-permute-start(f32[5,2,16,128]{3,2,1,0:T(8,128)} %get-tuple-element.82), channel_id=1, source_target_pairs={{0,1},{1,2},{2,3},{4,5},{5,6},{6,7},{8,9},{9,10},{10,11},{12,13},{... | collective-permute-start | bytes 245768 | tf_op jit(solution)/shard_map/ppermute | solution.py:22
  19.7 1.3 collective-permute-start.1
  21.0 1.2 fusion.115
  22.2 1.6 %fusion.113 = (f32[5,8,1,128]{3,2,1,0:T(1,128)}, f32[5,8,1,128]{3,2,1,0:T(1,128)}) fusion(f32[5,8,16,128]{3,2,1,0:T(8,128)} %param.5), kind=kLoop, calls=%fused_computation.304 | loop fusion | bytes 81920 | tf_op jit(solution)/shard_map/slice | solution.py:132
  23.9 0.3 copy.62
  24.2 0.3 copy.63
  24.5 0.2 reshape.105
  24.7 0.1 reshape.106
  24.8 0.3 pad_maximum_fusion.7
  25.4 1.1 fusion.16
  26.5 2.9 %multiply_sine_fusion.3 = (f32[24,4,128]{2,1,0:T(4,128)S(1)}, f32[24,4,128]{2,1,0:T(4,128)S(1)}, f32[24,4,128]{2,1,0:T(4,128)S(1)}, f32[24,4,128]{2,1,0:T(4,128)...) fusion(f32[4,128]{1,0:T(4,128)S(1)} %get-tuple-element.128, ...), kind=kLoop, calls=%fused_computation.246 | loop fusion | flops 184320 | bytes 604352 | tf_op jit(solution)/shard_map/sin | solution.py:72
  29.4 0.4 fusion.43
  29.8 0.6 bitcast_add_fusion
  30.5 14.3 %all_gather.6 = f32[10,16,128]{2,0,1:T(8,128)S(1)} all-gather(f32[10,4,128]{2,0,1:T(8,128)S(1)} %copy.52), channel_id=1, replica_groups=mesh['blk'=8,'pitch'=4] {'pitch'}, dimensions={1}, use_global_device_ids=true | all-gather | bytes 102400 | tf_op jit(solution)/shard_map/all_gather | solution.py:113
  44.8 0.7 copy.54
  45.6 13.3 %all_gather.7 = f32[10,16,128]{2,0,1:T(8,128)S(1)} all-gather(f32[10,4,128]{2,0,1:T(8,128)S(1)} %copy.54), channel_id=1, replica_groups=mesh['blk'=8,'pitch'=4] {'pitch'}, dimensions={1}, use_global_device_ids=true | all-gather | bytes 102400 | tf_op jit(solution)/shard_map/all_gather | solution.py:114
  59.0 0.8 broadcast_select_fusion.5
  59.7 0.8 broadcast_select_fusion.2
  60.8 0.4 fusion.37
  61.2 0.9 broadcast_select_fusion.8
  62.3 0.1 fusion.71
  62.5 0.7 copy-done.2
  63.2 0.2 fusion.93
  63.4 0.4 slice_reduce_fusion.2
  63.8 0.1 reshape.107
  64.0 0.1 reshape.108
  64.1 0.3 pad_maximum_fusion.8
  64.7 1.1 fusion.9
  65.8 1.3 collective-permute-start.6
  67.1 1.3 collective-permute-start.7
  68.4 4.8 %collective-permute-start.4 = (f32[5,2,16,128]{3,2,1,0:T(8,128)S(1)}, f32[5,2,16,128]{3,2,1,0:T(8,128)S(1)}, u32[]{:S(2)}, u32[]{:S(2)}) collective-permute-start(f32[5,2,16,128]{3,2,1,0:T(8,128)S(1)} %get-tuple-element.76), channel_id=1, source_target_pairs={{0,1},{1,2},{2,3},{4,5},{5,6},{6,7},{8,9},{9,10},{10,11},{12,13},{... | collective-permute-start | bytes 245768 | tf_op jit(solution)/shard_map/ppermute | solution.py:22
  73.2 1.3 collective-permute-start.5
  74.8 0.4 fusion.30
  75.3 4.3 %collective-permute-done.5 = f32[5,2,16,128]{3,2,1,0:T(8,128)S(1)} collective-permute-done((f32[5,2,16,128]{3,2,1,0:T(8,128)S(1)}, f32[5,2,16,128]{3,2,1,0:T(8,128)S(1)}, u32[]{:S(2)}, u32[]{:S(2)}) %collective-permute-start.5) | collective-permute-done | bytes 81952 | tf_op jit(solution)/shard_map/ppermute | solution.py:25
  79.8 0.1 fusion.63
  79.9 0.2 fusion.88
  80.1 0.4 slice_reduce_fusion
  80.6 0.1 reshape.109
  80.7 0.1 reshape.110
  80.9 0.3 pad_maximum_fusion.9
  81.4 1.1 fusion.2
  82.5 5.2 %collective-permute-start.10 = (f32[5,8,2,128]{3,2,1,0:T(2,128)S(1)}, f32[5,8,2,128]{3,2,1,0:T(2,128)S(1)}, u32[]{:S(2)}, u32[]{:S(2)}) collective-permute-start(f32[5,8,2,128]{3,2,1,0:T(2,128)S(1)} %get-tuple-element.74), channel_id=1, source_target_pairs={{0,4},{4,8},{8,12},{12,16},{16,20},{20,24},{24,28},{1,5},{5,9},{9,... | collective-permute-start | bytes 122888 | tf_op jit(solution)/shard_map/ppermute | solution.py:22
  87.7 1.3 collective-permute-start.11
  89.0 2.3 %collective-permute-start.8 = (f32[5,2,16,128]{3,2,1,0:T(8,128)S(1)}, f32[5,2,16,128]{3,2,1,0:T(8,128)S(1)}, u32[]{:S(2)}, u32[]{:S(2)}) collective-permute-start(f32[5,2,16,128]{3,2,1,0:T(8,128)S(1)} %get-tuple-element.70), channel_id=1, source_target_pairs={{0,1},{1,2},{2,3},{4,5},{5,6},{6,7},{8,9},{9,10},{10,11},{12,13},{... | collective-permute-start | bytes 245768 | tf_op jit(solution)/shard_map/ppermute | solution.py:22
  91.3 1.5 collective-permute-start.9
  92.8 1.4 collective-permute-done.11
  94.5 0.4 fusion.23
  94.9 2.8 %collective-permute-done.9 = f32[5,2,16,128]{3,2,1,0:T(8,128)S(1)} collective-permute-done((f32[5,2,16,128]{3,2,1,0:T(8,128)S(1)}, f32[5,2,16,128]{3,2,1,0:T(8,128)S(1)}, u32[]{:S(2)}, u32[]{:S(2)}) %collective-permute-start.9) | collective-permute-done | bytes 81952 | tf_op jit(solution)/shard_map/ppermute | solution.py:25
  98.0 0.3 fusion.83
  98.3 0.7 slice_select_fusion.1
  99.1 0.6 dynamic-slice
  100.3 39.2 %all-reduce.5.cloned.1.call-done = (f32[10,16,128]{2,1,0:T(8,128)}, f32[10,16,128]{2,1,0:T(8,128)}) async-done(((f32[10,16,128]{2,1,0:T(8,128)}, f32[10,16,128]{2,1,0:T(8,128)}), (f32[10,16,128]{2,1,0:T(8,128)}, f32[10,16,128]{2,1,0:T(8,128)})) %all-reduce.5.cloned.1.call-update) | async-done | bytes 163856
  139.4 0.8 dynamic-slice_multiply_fusion.1
  140.2 0.8 dynamic-slice_multiply_fusion
  141.0 0.9 add_reduce_fusion.1
  142.0 0.8 add_bitcast_fusion.1
  142.8 0.2 maximum_bitcast_fusion.1
  143.0 0.2 maximum_bitcast_fusion
  143.3 1.8 %pad_maximum_fusion = f32[2,49,10,4,128]{4,3,2,1,0:T(4,128)} fusion(f32[1,49,10,4,128]{4,3,2,1,0:T(4,128)S(1)} %maximum_bitcast_fusion.1, f32[1,49,10,4,128]{4,3,2,1,0:T(4,128)S(1)} %maximum_bitcast_fusion), kind=kLoop, calls=%fused_computation | loop fusion | flops 501760 | bytes 4014080 | tf_op jit(solution)/shard_map/stack | solution.py:169
  145.0 0.6 pad_maximum_fusion.28
  (99 shorter events, 2.2 us)
Async XLA Ops:
  7.2 17.6 %copy-start = (f32[5,8,16,128]{3,2,1,0:T(8,128)S(1)}, f32[5,8,16,128]{3,2,1,0:T(8,128)}, u32[]{:S(2)}) copy-start(f32[5,8,16,128]{3,2,1,0:T(8,128)} %param.5) | copy-start | bytes 983044
  7.2 132.3 %all-reduce.5.cloned.1.call-start = ((), (), s32[]{:S(2)}) async-start(), calls=%async_computation | async-start | bytes 327680
  8.9 50.1 %collective-permute-start.2 = (f32[5,8,2,128]{3,2,1,0:T(2,128)}, f32[5,8,2,128]{3,2,1,0:T(2,128)}, u32[]{:S(2)}, u32[]{:S(2)}) collective-permute-start(f32[5,8,2,128]{3,2,1,0:T(2,128)} %get-tuple-element.86), channel_id=1, source_target_pairs={{0,4},{4,8},{8,12},{12,16},{16,20},{20,24},{24,28},{1,5},{5,9},{9,... | collective-permute-start | bytes 122888 | tf_op jit(solution)/shard_map/ppermute | solution.py:22
  11.9 47.8 %collective-permute-start.3 = (f32[5,8,2,128]{3,2,1,0:T(2,128)}, f32[5,8,2,128]{3,2,1,0:T(2,128)}, u32[]{:S(2)}, u32[]{:S(2)}) collective-permute-start(f32[5,8,2,128]{3,2,1,0:T(2,128)} %get-tuple-element.85), channel_id=1, source_target_pairs={{4,0},{8,4},{12,8},{16,12},{20,16},{24,20},{28,24},{5,1},{9,5},{13... | collective-permute-start | bytes 122888 | tf_op jit(solution)/shard_map/ppermute | solution.py:25
  14.8 46.4 %collective-permute-start = (f32[5,2,16,128]{3,2,1,0:T(8,128)}, f32[5,2,16,128]{3,2,1,0:T(8,128)}, u32[]{:S(2)}, u32[]{:S(2)}) collective-permute-start(f32[5,2,16,128]{3,2,1,0:T(8,128)} %get-tuple-element.82), channel_id=1, source_target_pairs={{0,1},{1,2},{2,3},{4,5},{5,6},{6,7},{8,9},{9,10},{10,11},{12,13},{... | collective-permute-start | bytes 245768 | tf_op jit(solution)/shard_map/ppermute | solution.py:22
  19.7 41.5 %collective-permute-start.1 = (f32[5,2,16,128]{3,2,1,0:T(8,128)}, f32[5,2,16,128]{3,2,1,0:T(8,128)}, u32[]{:S(2)}, u32[]{:S(2)}) collective-permute-start(f32[5,2,16,128]{3,2,1,0:T(8,128)} %get-tuple-element.81), channel_id=1, source_target_pairs={{1,0},{2,1},{3,2},{5,4},{6,5},{7,6},{9,8},{10,9},{11,10},{13,12},{... | collective-permute-start | bytes 245768 | tf_op jit(solution)/shard_map/ppermute | solution.py:25
  25.2 1.2 copy-start.5
  25.3 1.2 copy-start.6
  25.3 4.1 %copy-start.1 = (f32[2,49,10,4,128]{4,3,2,1,0:T(4,128)S(1)}, f32[2,49,10,4,128]{4,3,2,1,0:T(4,128)}, u32[]{:S(2)}) copy-start(f32[2,49,10,4,128]{4,3,2,1,0:T(4,128)} %param.7) | copy-start | bytes 6021124
  62.2 1.0 copy-start.2
  65.8 8.8 %collective-permute-start.6 = (f32[5,8,2,128]{3,2,1,0:T(2,128)S(1)}, f32[5,8,2,128]{3,2,1,0:T(2,128)S(1)}, u32[]{:S(2)}, u32[]{:S(2)}) collective-permute-start(f32[5,8,2,128]{3,2,1,0:T(2,128)S(1)} %get-tuple-element.80), channel_id=1, source_target_pairs={{0,4},{4,8},{8,12},{12,16},{16,20},{20,24},{24,28},{1,5},{5,9},{9,... | collective-permute-start | bytes 122888 | tf_op jit(solution)/shard_map/ppermute | solution.py:22
  67.1 7.5 %collective-permute-start.7 = (f32[5,8,2,128]{3,2,1,0:T(2,128)S(1)}, f32[5,8,2,128]{3,2,1,0:T(2,128)S(1)}, u32[]{:S(2)}, u32[]{:S(2)}) collective-permute-start(f32[5,8,2,128]{3,2,1,0:T(2,128)S(1)} %get-tuple-element.79), channel_id=1, source_target_pairs={{4,0},{8,4},{12,8},{16,12},{20,16},{24,20},{28,24},{5,1},{9,5},{13... | collective-permute-start | bytes 122888 | tf_op jit(solution)/shard_map/ppermute | solution.py:25
  68.4 6.9 %collective-permute-start.4 = (f32[5,2,16,128]{3,2,1,0:T(8,128)S(1)}, f32[5,2,16,128]{3,2,1,0:T(8,128)S(1)}, u32[]{:S(2)}, u32[]{:S(2)}) collective-permute-start(f32[5,2,16,128]{3,2,1,0:T(8,128)S(1)} %get-tuple-element.76), channel_id=1, source_target_pairs={{0,1},{1,2},{2,3},{4,5},{5,6},{6,7},{8,9},{9,10},{10,11},{12,13},{... | collective-permute-start | bytes 245768 | tf_op jit(solution)/shard_map/ppermute | solution.py:22
  73.2 6.3 %collective-permute-start.5 = (f32[5,2,16,128]{3,2,1,0:T(8,128)S(1)}, f32[5,2,16,128]{3,2,1,0:T(8,128)S(1)}, u32[]{:S(2)}, u32[]{:S(2)}) collective-permute-start(f32[5,2,16,128]{3,2,1,0:T(8,128)S(1)} %get-tuple-element.75), channel_id=1, source_target_pairs={{1,0},{2,1},{3,2},{5,4},{6,5},{7,6},{9,8},{10,9},{11,10},{13,12},{... | collective-permute-start | bytes 245768 | tf_op jit(solution)/shard_map/ppermute | solution.py:25
  82.5 10.3 %collective-permute-start.10 = (f32[5,8,2,128]{3,2,1,0:T(2,128)S(1)}, f32[5,8,2,128]{3,2,1,0:T(2,128)S(1)}, u32[]{:S(2)}, u32[]{:S(2)}) collective-permute-start(f32[5,8,2,128]{3,2,1,0:T(2,128)S(1)} %get-tuple-element.74), channel_id=1, source_target_pairs={{0,4},{4,8},{8,12},{12,16},{16,20},{20,24},{24,28},{1,5},{5,9},{9,... | collective-permute-start | bytes 122888 | tf_op jit(solution)/shard_map/ppermute | solution.py:22
  87.7 6.5 %collective-permute-start.11 = (f32[5,8,2,128]{3,2,1,0:T(2,128)S(1)}, f32[5,8,2,128]{3,2,1,0:T(2,128)S(1)}, u32[]{:S(2)}, u32[]{:S(2)}) collective-permute-start(f32[5,8,2,128]{3,2,1,0:T(2,128)S(1)} %get-tuple-element.73), channel_id=1, source_target_pairs={{4,0},{8,4},{12,8},{16,12},{20,16},{24,20},{28,24},{5,1},{9,5},{13... | collective-permute-start | bytes 122888 | tf_op jit(solution)/shard_map/ppermute | solution.py:25
  89.0 5.8 %collective-permute-start.8 = (f32[5,2,16,128]{3,2,1,0:T(8,128)S(1)}, f32[5,2,16,128]{3,2,1,0:T(8,128)S(1)}, u32[]{:S(2)}, u32[]{:S(2)}) collective-permute-start(f32[5,2,16,128]{3,2,1,0:T(8,128)S(1)} %get-tuple-element.70), channel_id=1, source_target_pairs={{0,1},{1,2},{2,3},{4,5},{5,6},{6,7},{8,9},{9,10},{10,11},{12,13},{... | collective-permute-start | bytes 245768 | tf_op jit(solution)/shard_map/ppermute | solution.py:22
  91.3 6.3 %collective-permute-start.9 = (f32[5,2,16,128]{3,2,1,0:T(8,128)S(1)}, f32[5,2,16,128]{3,2,1,0:T(8,128)S(1)}, u32[]{:S(2)}, u32[]{:S(2)}) collective-permute-start(f32[5,2,16,128]{3,2,1,0:T(8,128)S(1)} %get-tuple-element.69), channel_id=1, source_target_pairs={{1,0},{2,1},{3,2},{5,4},{6,5},{7,6},{9,8},{10,9},{11,10},{13,12},{... | collective-permute-start | bytes 245768 | tf_op jit(solution)/shard_map/ppermute | solution.py:25
  98.0 1.1 copy-start.7
  98.0 43.0 %copy-start.4 = (f32[24,4,128]{2,1,0:T(4,128)S(1)}, f32[24,4,128]{2,1,0:T(4,128)}, u32[]{:S(2)}) copy-start(f32[24,4,128]{2,1,0:T(4,128)} %get-tuple-element.124) | copy-start | bytes 147460
  98.3 43.7 %copy-start.3 = (f32[5,8,16,128]{3,2,1,0:T(8,128)}, f32[5,8,16,128]{3,2,1,0:T(8,128)S(1)}, u32[]{:S(2)}) copy-start(f32[5,8,16,128]{3,2,1,0:T(8,128)S(1)} %fusion.83) | copy-start | bytes 983044
Sparse Core Ops, SparseCore 0:
  99.2 40.2 all-reduce.4
where the time goes:
time: 153 us; the launch traced here: 152 us
  waiting for transfers between devices  47.7 us (31%)
  starting transfers between devices  29.4 us (19%)
  blocking collectives  27.7 us (18%)
  other arithmetic  21.4 us (14%)
  between operations  15.5 us (10%)
  local copies, waits for them, and re-layouts  10.7 us (7%)
    unnamed x2, waiting for transfers between devices  39.2 us
    ppermute x6, starting transfers between devices, padded_2(): lax.ppermute(lax.slice_in_dim(block, block.shape[dim] - width, None, axis...  21.5 us
    all_gather x1, blocking collectives, shards(): lax.all_gather(low_share, 'pitch', axis=1, tiled=True)  14.3 us
    all_gather x1, blocking collectives, shards(): lax.all_gather(high_share, 'pitch', axis=1, tiled=True)  13.3 us
    ppermute x6, waiting for transfers between devices, padded_2(): lax.ppermute(lax.slice_in_dim(block, 0, width, axis=dim), axis, backward)  8.44 us
    ppermute x6, starting transfers between devices, padded_2(): lax.ppermute(lax.slice_in_dim(block, 0, width, axis=dim), axis, backward)  7.91 us
    sub x9, other arithmetic, face_sum(): 0.5 * (window(cell_flux, 1, faces_n) + window(cell_flux, 2, faces_n))  4.7 us
    slice x6, local copies, waits for them, and re-layouts, padded_2(): lax.slice_in_dim(block, 0, width, axis=dim)  3.38 us
  transfers between devices with their start and end apart: 13, of which 5 were waited for; matrix products, arithmetic and copies ran while one was open for 10% of the time, Pallas kernels for 0%

commit v1 on v0

--- a/solution.py
+++ b/solution.py
@@ -12,6 +12,16 @@
 physical_step = 0.25
 relax_rate = 0.125
 lag_turns = 0.3
+
+
+def collect(x, axis, dim):
+    ways, here, hop = (lax.axis_size(axis), lax.axis_index(axis), x.shape[dim])
+    lengths = [n * ways if d == dim else n for d, n in enumerate(x.shape)]
+    full = lax.dynamic_update_slice_in_dim(jnp.zeros(lengths, x.dtype), x, here * hop, axis=dim)
+    for far in range(1, ways):
+        x = lax.ppermute(x, axis, [(d, (d + 1) % ways) for d in range(ways)])
+        full = lax.dynamic_update_slice_in_dim(full, x, (here - far) % ways * hop, axis=dim)
+    return full
 
 
 def padded_2(block, sides, width):
@@ -111,7 +121,7 @@
     high_share = rebuild(fourier_store[1], phases[1] + phase_lag, harmonics)
     low_whole, high_whole = (
         lax.all_gather(low_share, "pitch", axis=1, tiled=True),
-        lax.all_gather(high_share, "pitch", axis=1, tiled=True),
+        collect(high_share, "pitch", 1),
     )
     ghost_shape = (5, 2, block_rows, radial_cells)
     low_ghost = low_whole.reshape(ghost_shape)

time: 153 us -> 146 us (0.954)
  blocking collectives: 27.7 us -> 14.9 us
  waiting for transfers between devices: 47.7 us -> 54.5 us
  other arithmetic: 21.4 us -> 23.6 us
  local copies, waits for them, and re-layouts: 10.7 us -> 8.8 us
  starting transfers between devices: 29.4 us -> 27.5 us
    all_gather x1 -> x0, blocking collectives: 13.3 us -> none  [shards(): lax.all_gather(high_share, 'pitch', axis=1, tiled=True)]
    ppermute x0 -> x3, waiting for transfers between devices: none -> 7.97 us  [collect(): x = lax.ppermute(x, axis, [(d, (d + 1) % ways) for d in range(ways)])]
    ppermute x6, starting transfers between devices: 21.5 us -> 18.1 us  [padded_2(): lax.ppermute(lax.slice_in_dim(block, block.shape[dim] - width, None, axis...]
  transfers between devices with their start and end apart: 13 -> 16, of which waited for: 5 -> 7; matrix products, arithmetic and copies ran while one was open for 10% -> 11% of each run, Pallas kernels for 0% -> 0%
where the time goes in v1:
time: 146 us; the launch traced here: 145 us
  waiting for transfers between devices  54.5 us (37%)
  starting transfers between devices  27.5 us (19%)
  other arithmetic  23.6 us (16%)
  between operations  15.5 us (11%)
  blocking collectives  14.9 us (10%)
  local copies, waits for them, and re-layouts  8.8 us (6%)
    unnamed x2, waiting for transfers between devices  38.1 us
    ppermute x6, starting transfers between devices, padded_2(): lax.ppermute(lax.slice_in_dim(block, block.shape[dim] - width, None, axis...  18.1 us
    all_gather x1, blocking collectives, shards(): lax.all_gather(low_share, 'pitch', axis=1, tiled=True)  14.9 us
    ppermute x6, waiting for transfers between devices, padded_2(): lax.ppermute(lax.slice_in_dim(block, 0, width, axis=dim), axis, backward)  8.49 us
    ppermute x3, waiting for transfers between devices, collect(): x = lax.ppermute(x, axis, [(d, (d + 1) % ways) for d in range(ways)])  7.97 us
    ppermute x6, starting transfers between devices, padded_2(): lax.ppermute(lax.slice_in_dim(block, 0, width, axis=dim), axis, backward)  7.91 us
    sub x9, other arithmetic, face_sum(): 0.5 * (window(cell_flux, 1, faces_n) + window(cell_flux, 2, faces_n))  4.71 us
    slice x6, local copies, waits for them, and re-layouts, padded_2(): lax.slice_in_dim(block, 0, width, axis=dim)  3.5 us
  transfers between devices with their start and end apart: 16, of which 7 were waited for; matrix products, arithmetic and copies ran while one was open for 11% of the time, Pallas kernels for 0%

profile of v1, /device:TPU:0, one launch (start us, length us, event | category | flops | bytes accessed | tf_op | source)
XLA Modules:
  0.0 144.9 jit_solution(6735472753304272070)
XLA Ops:
  7.2 1.8 %fusion.114 = (f32[5,8,2,128]{3,2,1,0:T(2,128)}, f32[5,8,2,128]{3,2,1,0:T(2,128)}) fusion(f32[5,8,16,128]{3,2,1,0:T(8,128)} %param.5), kind=kLoop, calls=%fused_computation.309 | loop fusion | bytes 163840 | tf_op jit(solution)/shard_map/slice | solution.py:35
  9.0 3.0 %collective-permute-start.5 = (f32[5,8,2,128]{3,2,1,0:T(2,128)}, f32[5,8,2,128]{3,2,1,0:T(2,128)}, u32[]{:S(2)}, u32[]{:S(2)}) collective-permute-start(f32[5,8,2,128]{3,2,1,0:T(2,128)} %get-tuple-element.84), channel_id=1, source_target_pairs={{0,4},{4,8},{8,12},{12,16},{16,20},{20,24},{24,28},{1,5},{5,9},{9,... | collective-permute-start | bytes 122888 | tf_op jit(solution)/shard_map/ppermute | solution.py:32
  12.0 1.3 collective-permute-start.6
  13.3 1.6 %fusion.112 = (f32[5,2,16,128]{3,2,1,0:T(8,128)}, f32[5,2,16,128]{3,2,1,0:T(8,128)}) fusion(f32[5,8,16,128]{3,2,1,0:T(8,128)} %param.5), kind=kLoop, calls=%fused_computation.307 | loop fusion | bytes 327680 | tf_op jit(solution)/shard_map/slice | solution.py:35
  14.9 4.9 %collective-permute-start = (f32[5,2,16,128]{3,2,1,0:T(8,128)}, f32[5,2,16,128]{3,2,1,0:T(8,128)}, u32[]{:S(2)}, u32[]{:S(2)}) collective-permute-start(f32[5,2,16,128]{3,2,1,0:T(8,128)} %get-tuple-element.80), channel_id=1, source_target_pairs={{0,1},{1,2},{2,3},{4,5},{5,6},{6,7},{8,9},{9,10},{10,11},{12,13},{... | collective-permute-start | bytes 245768 | tf_op jit(solution)/shard_map/ppermute | solution.py:32
  19.9 0.7 broadcast_add_fusion
  20.5 2.9 %multiply_sine_fusion.3 = (f32[24,4,128]{2,1,0:T(4,128)S(1)}, f32[24,4,128]{2,1,0:T(4,128)S(1)}, f32[24,4,128]{2,1,0:T(4,128)S(1)}, f32[24,4,128]{2,1,0:T(4,128)...) fusion(f32[4,128]{1,0:T(4,128)S(1)} %get-tuple-element.126, ...), kind=kLoop, calls=%fused_computation.246 | loop fusion | flops 184320 | bytes 604352 | tf_op jit(solution)/shard_map/sin | solution.py:82
  23.5 1.9 %fusion.43 = (f32[10,4,128]{2,1,0:T(4,128)S(1)}, f32[10,4,128]{2,1,0:T(4,128)S(1)}) fusion(f32[2,49,10,4,128]{4,3,2,1,0:T(4,128)} %param.7, f32[24,4,128]{2,1,0:T(4,128)S(1)} %get-tuple-element.118, f32[24,4,128]{2,1,0:T(4,128)S(1)} %get-tuple-element.117, f32[24,4,128]{2,1,0:T(4,128)S(1)} %get-tuple-element.114, f32[24,4,128]{2,1,0:T(4,128)S(1)} %get-tuple-element.113), kind=kLoop, calls=%fused_computation.81 | loop fusion | flops 972800 | bytes 2203648 | tf_op jit(solution)/shard_map/reduce_sum | solution.py:94
  25.4 0.6 constant_dynamic-update-slice_fusion.9
  26.1 1.0 collective-permute-start.1
  27.1 1.3 collective-permute-start.4
  28.3 0.2 fusion.115
  28.5 0.6 fusion.113
  29.2 0.3 copy.52
  29.4 0.3 copy.53
  29.7 0.2 reshape.105
  29.9 0.1 reshape.106
  30.1 0.3 pad_maximum_fusion.7
  30.6 1.1 fusion.16
  31.7 14.9 %all_gather.3 = f32[10,16,128]{2,0,1:T(8,128)S(1)} all-gather(f32[10,4,128]{2,0,1:T(8,128)S(1)} %copy.44), channel_id=1, replica_groups=mesh['blk'=8,'pitch'=4] {'pitch'}, dimensions={1}, use_global_device_ids=true | all-gather | bytes 102400 | tf_op jit(solution)/shard_map/all_gather | solution.py:123
  46.7 0.5 collective-permute-start.2
  47.2 0.8 constant_dynamic-update-slice_fusion.8
  48.0 0.8 broadcast_select_fusion.5
  48.7 0.8 broadcast_select_fusion.2
  49.8 0.4 fusion.37
  50.2 2.4 %collective-permute-done.2 = f32[10,4,128]{2,1,0:T(4,128)S(1)} collective-permute-done((f32[10,4,128]{2,1,0:T(4,128)}, f32[10,4,128]{2,1,0:T(4,128)S(1)}, u32[]{:S(2)}, u32[]{:S(2)}) %collective-permute-start.2) | collective-permute-done | bytes 20512 | tf_op jit(solution)/shard_map/ppermute | solution.py:22
  52.6 5.6 %collective-permute-done.3 = f32[10,4,128]{2,1,0:T(4,128)S(1)} collective-permute-done((f32[10,4,128]{2,1,0:T(4,128)S(1)}, f32[10,4,128]{2,1,0:T(4,128)S(1)}, u32[]{:S(2)}, u32[]{:S(2)}) %collective-permute-start.3) | collective-permute-done | bytes 20512 | tf_op jit(solution)/shard_map/ppermute | solution.py:22
  58.2 0.9 broadcast_select_fusion.8
  59.4 0.7 copy-done.2
  60.1 0.3 fusion.93
  60.4 0.4 slice_reduce_fusion.2
  61.0 0.1 reshape.108
  61.1 0.3 pad_maximum_fusion.8
  61.6 1.1 fusion.9
  62.7 1.3 collective-permute-start.9
  64.1 1.3 collective-permute-start.10
  65.4 1.3 collective-permute-start.7
  66.7 1.3 collective-permute-start.8
  68.0 2.5 %collective-permute-done.10 = f32[5,8,2,128]{3,2,1,0:T(2,128)S(1)} collective-permute-done((f32[5,8,2,128]{3,2,1,0:T(2,128)S(1)}, f32[5,8,2,128]{3,2,1,0:T(2,128)S(1)}, u32[]{:S(2)}, u32[]{:S(2)}) %collective-permute-start.10) | collective-permute-done | bytes 40992 | tf_op jit(solution)/shard_map/ppermute | solution.py:35
  70.8 0.4 fusion.30
  71.2 1.8 %collective-permute-done.8 = f32[5,2,16,128]{3,2,1,0:T(8,128)S(1)} collective-permute-done((f32[5,2,16,128]{3,2,1,0:T(8,128)S(1)}, f32[5,2,16,128]{3,2,1,0:T(8,128)S(1)}, u32[]{:S(2)}, u32[]{:S(2)}) %collective-permute-start.8) | collective-permute-done | bytes 81952 | tf_op jit(solution)/shard_map/ppermute | solution.py:35
  73.3 0.2 fusion.88
  73.6 0.4 slice_reduce_fusion
  74.3 0.3 pad_maximum_fusion.9
  74.9 1.1 fusion.2
  75.9 5.2 %collective-permute-start.13 = (f32[5,8,2,128]{3,2,1,0:T(2,128)S(1)}, f32[5,8,2,128]{3,2,1,0:T(2,128)S(1)}, u32[]{:S(2)}, u32[]{:S(2)}) collective-permute-start(f32[5,8,2,128]{3,2,1,0:T(2,128)S(1)} %get-tuple-element.72), channel_id=1, source_target_pairs={{0,4},{4,8},{8,12},{12,16},{16,20},{20,24},{24,28},{1,5},{5,9},{9,... | collective-permute-start | bytes 122888 | tf_op jit(solution)/shard_map/ppermute | solution.py:32
  81.2 1.3 collective-permute-start.14
  82.5 2.4 %collective-permute-start.11 = (f32[5,2,16,128]{3,2,1,0:T(8,128)S(1)}, f32[5,2,16,128]{3,2,1,0:T(8,128)S(1)}, u32[]{:S(2)}, u32[]{:S(2)}) collective-permute-start(f32[5,2,16,128]{3,2,1,0:T(8,128)S(1)} %get-tuple-element.68), channel_id=1, source_target_pairs={{0,1},{1,2},{2,3},{4,5},{5,6},{6,7},{8,9},{9,10},{10,11},{12,13},{... | collective-permute-start | bytes 245768 | tf_op jit(solution)/shard_map/ppermute | solution.py:32
  84.9 1.5 %collective-permute-start.12 = (f32[5,2,16,128]{3,2,1,0:T(8,128)S(1)}, f32[5,2,16,128]{3,2,1,0:T(8,128)S(1)}, u32[]{:S(2)}, u32[]{:S(2)}) collective-permute-start(f32[5,2,16,128]{3,2,1,0:T(8,128)S(1)} %get-tuple-element.67), channel_id=1, source_target_pairs={{1,0},{2,1},{3,2},{5,4},{6,5},{7,6},{9,8},{10,9},{11,10},{13,12},{... | collective-permute-start | bytes 245768 | tf_op jit(solution)/shard_map/ppermute | solution.py:35
  86.4 1.2 collective-permute-done.14
  87.8 0.4 fusion.23
  88.2 3.0 %collective-permute-done.12 = f32[5,2,16,128]{3,2,1,0:T(8,128)S(1)} collective-permute-done((f32[5,2,16,128]{3,2,1,0:T(8,128)S(1)}, f32[5,2,16,128]{3,2,1,0:T(8,128)S(1)}, u32[]{:S(2)}, u32[]{:S(2)}) %collective-permute-start.12) | collective-permute-done | bytes 81952 | tf_op jit(solution)/shard_map/ppermute | solution.py:35
  91.6 0.2 fusion.83
  91.8 0.7 slice_select_fusion.1
  92.6 0.6 dynamic-slice
  93.8 38.1 %all-reduce.5.cloned.1.call-done = (f32[10,16,128]{2,1,0:T(8,128)}, f32[10,16,128]{2,1,0:T(8,128)}) async-done(((f32[10,16,128]{2,1,0:T(8,128)}, f32[10,16,128]{2,1,0:T(8,128)}), (f32[10,16,128]{2,1,0:T(8,128)}, f32[10,16,128]{2,1,0:T(8,128)})) %all-reduce.5.cloned.1.call-update) | async-done | bytes 163856
  131.9 0.8 dynamic-slice_multiply_fusion.1
  132.7 0.8 dynamic-slice_multiply_fusion
  133.5 0.9 add_reduce_fusion.1
  134.4 0.8 add_bitcast_fusion.1
  135.2 0.2 maximum_bitcast_fusion.1
  135.5 0.2 maximum_bitcast_fusion
  135.7 1.8 %pad_maximum_fusion = f32[2,49,10,4,128]{4,3,2,1,0:T(4,128)} fusion(f32[1,49,10,4,128]{4,3,2,1,0:T(4,128)S(1)} %maximum_bitcast_fusion.1, f32[1,49,10,4,128]{4,3,2,1,0:T(4,128)S(1)} %maximum_bitcast_fusion), kind=kLoop, calls=%fused_computation | loop fusion | flops 501760 | bytes 4014080 | tf_op jit(solution)/shard_map/stack | solution.py:179
  137.4 0.6 pad_maximum_fusion.28
  (100 shorter events, 2.8 us)
Async XLA Ops:
  7.2 21.2 %copy-start = (f32[5,8,16,128]{3,2,1,0:T(8,128)S(1)}, f32[5,8,16,128]{3,2,1,0:T(8,128)}, u32[]{:S(2)}) copy-start(f32[5,8,16,128]{3,2,1,0:T(8,128)} %param.5) | copy-start | bytes 983044
  7.2 18.3 %copy-start.1 = (f32[2,49,10,4,128]{4,3,2,1,0:T(4,128)S(1)}, f32[2,49,10,4,128]{4,3,2,1,0:T(4,128)}, u32[]{:S(2)}) copy-start(f32[2,49,10,4,128]{4,3,2,1,0:T(4,128)} %param.7) | copy-start | bytes 6021124
  7.2 124.7 %all-reduce.5.cloned.1.call-start = ((), (), s32[]{:S(2)}) async-start(), calls=%async_computation | async-start | bytes 327680
  9.0 38.9 %collective-permute-start.5 = (f32[5,8,2,128]{3,2,1,0:T(2,128)}, f32[5,8,2,128]{3,2,1,0:T(2,128)}, u32[]{:S(2)}, u32[]{:S(2)}) collective-permute-start(f32[5,8,2,128]{3,2,1,0:T(2,128)} %get-tuple-element.84), channel_id=1, source_target_pairs={{0,4},{4,8},{8,12},{12,16},{16,20},{20,24},{24,28},{1,5},{5,9},{9,... | collective-permute-start | bytes 122888 | tf_op jit(solution)/shard_map/ppermute | solution.py:32
  12.0 36.7 %collective-permute-start.6 = (f32[5,8,2,128]{3,2,1,0:T(2,128)}, f32[5,8,2,128]{3,2,1,0:T(2,128)}, u32[]{:S(2)}, u32[]{:S(2)}) collective-permute-start(f32[5,8,2,128]{3,2,1,0:T(2,128)} %get-tuple-element.83), channel_id=1, source_target_pairs={{4,0},{8,4},{12,8},{16,12},{20,16},{24,20},{28,24},{5,1},{9,5},{13... | collective-permute-start | bytes 122888 | tf_op jit(solution)/shard_map/ppermute | solution.py:35
  14.9 43.2 %collective-permute-start = (f32[5,2,16,128]{3,2,1,0:T(8,128)}, f32[5,2,16,128]{3,2,1,0:T(8,128)}, u32[]{:S(2)}, u32[]{:S(2)}) collective-permute-start(f32[5,2,16,128]{3,2,1,0:T(8,128)} %get-tuple-element.80), channel_id=1, source_target_pairs={{0,1},{1,2},{2,3},{4,5},{5,6},{6,7},{8,9},{9,10},{10,11},{12,13},{... | collective-permute-start | bytes 245768 | tf_op jit(solution)/shard_map/ppermute | solution.py:32
  26.1 20.6 %collective-permute-start.1 = (f32[10,4,128]{2,1,0:T(4,128)}, f32[10,4,128]{2,1,0:T(4,128)}, u32[]{:S(2)}, u32[]{:S(2)}) collective-permute-start(f32[10,4,128]{2,1,0:T(4,128)} %get-tuple-element.46), channel_id=1, source_target_pairs={{0,1},{1,2},{2,3},{3,0},{4,5},{5,6},{6,7},{7,4},{8,9},{9,10},{10,1... | collective-permute-start | bytes 61448 | tf_op jit(solution)/shard_map/ppermute | solution.py:22
  27.1 31.1 %collective-permute-start.4 = (f32[5,2,16,128]{3,2,1,0:T(8,128)}, f32[5,2,16,128]{3,2,1,0:T(8,128)}, u32[]{:S(2)}, u32[]{:S(2)}) collective-permute-start(f32[5,2,16,128]{3,2,1,0:T(8,128)} %get-tuple-element.79), channel_id=1, source_target_pairs={{1,0},{2,1},{3,2},{5,4},{6,5},{7,6},{9,8},{10,9},{11,10},{13,12},{... | collective-permute-start | bytes 245768 | tf_op jit(solution)/shard_map/ppermute | solution.py:35
  46.7 5.8 %collective-permute-start.2 = (f32[10,4,128]{2,1,0:T(4,128)}, f32[10,4,128]{2,1,0:T(4,128)S(1)}, u32[]{:S(2)}, u32[]{:S(2)}) collective-permute-start(f32[10,4,128]{2,1,0:T(4,128)} %collective-permute-done.1), channel_id=1, source_target_pairs={{0,1},{1,2},{2,3},{3,0},{4,5},{5,6},{6,7},{7,4},{8,9},{9,10},{10,1... | collective-permute-start | bytes 61448 | tf_op jit(solution)/shard_map/ppermute | solution.py:22
  52.6 5.6 %collective-permute-start.3 = (f32[10,4,128]{2,1,0:T(4,128)S(1)}, f32[10,4,128]{2,1,0:T(4,128)S(1)}, u32[]{:S(2)}, u32[]{:S(2)}) collective-permute-start(f32[10,4,128]{2,1,0:T(4,128)S(1)} %collective-permute-done.2), channel_id=1, source_target_pairs={{0,1},{1,2},{2,3},{3,0},{4,5},{5,6},{6,7},{7,4},{8,9},{9,10},{10,1... | collective-permute-start | bytes 61448 | tf_op jit(solution)/shard_map/ppermute | solution.py:22
  59.2 1.0 copy-start.2
  62.7 5.2 %collective-permute-start.9 = (f32[5,8,2,128]{3,2,1,0:T(2,128)S(1)}, f32[5,8,2,128]{3,2,1,0:T(2,128)S(1)}, u32[]{:S(2)}, u32[]{:S(2)}) collective-permute-start(f32[5,8,2,128]{3,2,1,0:T(2,128)S(1)} %get-tuple-element.78), channel_id=1, source_target_pairs={{0,4},{4,8},{8,12},{12,16},{16,20},{20,24},{24,28},{1,5},{5,9},{9,... | collective-permute-start | bytes 122888 | tf_op jit(solution)/shard_map/ppermute | solution.py:32
  64.1 6.5 %collective-permute-start.10 = (f32[5,8,2,128]{3,2,1,0:T(2,128)S(1)}, f32[5,8,2,128]{3,2,1,0:T(2,128)S(1)}, u32[]{:S(2)}, u32[]{:S(2)}) collective-permute-start(f32[5,8,2,128]{3,2,1,0:T(2,128)S(1)} %get-tuple-element.77), channel_id=1, source_target_pairs={{4,0},{8,4},{12,8},{16,12},{20,16},{24,20},{28,24},{5,1},{9,5},{13... | collective-permute-start | bytes 122888 | tf_op jit(solution)/shard_map/ppermute | solution.py:35
  65.4 5.8 %collective-permute-start.7 = (f32[5,2,16,128]{3,2,1,0:T(8,128)S(1)}, f32[5,2,16,128]{3,2,1,0:T(8,128)S(1)}, u32[]{:S(2)}, u32[]{:S(2)}) collective-permute-start(f32[5,2,16,128]{3,2,1,0:T(8,128)S(1)} %get-tuple-element.74), channel_id=1, source_target_pairs={{0,1},{1,2},{2,3},{4,5},{5,6},{6,7},{8,9},{9,10},{10,11},{12,13},{... | collective-permute-start | bytes 245768 | tf_op jit(solution)/shard_map/ppermute | solution.py:32
  66.7 6.3 %collective-permute-start.8 = (f32[5,2,16,128]{3,2,1,0:T(8,128)S(1)}, f32[5,2,16,128]{3,2,1,0:T(8,128)S(1)}, u32[]{:S(2)}, u32[]{:S(2)}) collective-permute-start(f32[5,2,16,128]{3,2,1,0:T(8,128)S(1)} %get-tuple-element.73), channel_id=1, source_target_pairs={{1,0},{2,1},{3,2},{5,4},{6,5},{7,6},{9,8},{10,9},{11,10},{13,12},{... | collective-permute-start | bytes 245768 | tf_op jit(solution)/shard_map/ppermute | solution.py:35
  75.9 10.4 %collective-permute-start.13 = (f32[5,8,2,128]{3,2,1,0:T(2,128)S(1)}, f32[5,8,2,128]{3,2,1,0:T(2,128)S(1)}, u32[]{:S(2)}, u32[]{:S(2)}) collective-permute-start(f32[5,8,2,128]{3,2,1,0:T(2,128)S(1)} %get-tuple-element.72), channel_id=1, source_target_pairs={{0,4},{4,8},{8,12},{12,16},{16,20},{20,24},{24,28},{1,5},{5,9},{9,... | collective-permute-start | bytes 122888 | tf_op jit(solution)/shard_map/ppermute | solution.py:32
  81.2 6.4 %collective-permute-start.14 = (f32[5,8,2,128]{3,2,1,0:T(2,128)S(1)}, f32[5,8,2,128]{3,2,1,0:T(2,128)S(1)}, u32[]{:S(2)}, u32[]{:S(2)}) collective-permute-start(f32[5,8,2,128]{3,2,1,0:T(2,128)S(1)} %get-tuple-element.71), channel_id=1, source_target_pairs={{4,0},{8,4},{12,8},{16,12},{20,16},{24,20},{28,24},{5,1},{9,5},{13... | collective-permute-start | bytes 122888 | tf_op jit(solution)/shard_map/ppermute | solution.py:35
  82.5 5.7 %collective-permute-start.11 = (f32[5,2,16,128]{3,2,1,0:T(8,128)S(1)}, f32[5,2,16,128]{3,2,1,0:T(8,128)S(1)}, u32[]{:S(2)}, u32[]{:S(2)}) collective-permute-start(f32[5,2,16,128]{3,2,1,0:T(8,128)S(1)} %get-tuple-element.68), channel_id=1, source_target_pairs={{0,1},{1,2},{2,3},{4,5},{5,6},{6,7},{8,9},{9,10},{10,11},{12,13},{... | collective-permute-start | bytes 245768 | tf_op jit(solution)/shard_map/ppermute | solution.py:32
  84.9 6.3 %collective-permute-start.12 = (f32[5,2,16,128]{3,2,1,0:T(8,128)S(1)}, f32[5,2,16,128]{3,2,1,0:T(8,128)S(1)}, u32[]{:S(2)}, u32[]{:S(2)}) collective-permute-start(f32[5,2,16,128]{3,2,1,0:T(8,128)S(1)} %get-tuple-element.67), channel_id=1, source_target_pairs={{1,0},{2,1},{3,2},{5,4},{6,5},{7,6},{9,8},{10,9},{11,10},{13,12},{... | collective-permute-start | bytes 245768 | tf_op jit(solution)/shard_map/ppermute | solution.py:35
  91.6 1.0 copy-start.4
  91.8 42.6 %copy-start.3 = (f32[5,8,16,128]{3,2,1,0:T(8,128)}, f32[5,8,16,128]{3,2,1,0:T(8,128)S(1)}, u32[]{:S(2)}) copy-start(f32[5,8,16,128]{3,2,1,0:T(8,128)S(1)} %fusion.83) | copy-start | bytes 983044
Sparse Core Ops, SparseCore 0:
  92.7 39.1 all-reduce.4
